TPU v7x, 256 devices: a whole 4x4x8 slice. The times are simulated.
256 devices in a mesh: seq: 32 (over z, y_hi, core), tp: 8 (over y_lo, x).
Axes of the slice: x: 4, y: 4 (y_hi: 2, y_lo: 2; y = y_hi * 2 + y_lo), z: 8, core: 2. Of those that a mesh axis runs over, the one named last changes fastest.
Arguments:
- queries: bfloat16 [8192, 5120], P('seq', 'tp'), may hold values from -120 to 120, as said below
- prompt_keys: bfloat16 [4096, 1024], P('seq', 'tp'), may hold values from -4 to 4
- prompt_values: bfloat16 [4096, 1024], P('seq', 'tp'), may hold values from -6 to 6
- response_keys: bfloat16 [8192, 1024], P('seq', 'tp'), may hold values from -6 to 6
- response_values: bfloat16 [8192, 1024], P('seq', 'tp'), may hold values from -6 to 6
- lengths: int32 [16], replicated, may hold values from 1 to 4096, 8192 in all
- out_weight: bfloat16 [5120, 5120], P('tp'), may hold values from -0.125 to 0.125
Outputs:
- projected: bfloat16 [8192, 5120], P('seq', 'tp')
Inputs may be any that keep to these rules, and one draw needn't show every extreme that they name: `queries`: in a few rows a query head may be a multiple of a prompt key of its key head. 16 lengths that sum to 8192; the longest has exactly 4096 tokens.
All inputs are finite; a program needn't handle non-finite values.
Results may differ from a plain program's by a relative error of at most 0.014.
Values may be sent and summed in bfloat16 or wider, within the bound.
A program may use at most 192 MiB of HBM per device.

v0:
```python
import jax
import jax.numpy as jnp
from jax import lax
from jax.sharding import PartitionSpec as P

HEADS = 40
KVH = 8
HD = 128


def segment_layout(lengths, first_row, row_count):
    positions = first_row + jnp.arange(row_count, dtype=jnp.int32)
    seg_ends = jnp.cumsum(lengths)
    seg_starts = seg_ends - lengths
    inside = (positions[:, None] >= seg_starts[None, :]) & (positions[:, None] < seg_ends[None, :])
    own_start = jnp.sum(jnp.where(inside, seg_starts[None, :], 0), axis=1)
    return (positions, own_start)


def update_state(running, grouped, key_block, value_block, visible, scale_factor):
    maximum, summed, weighted = running
    scores = (
        jnp.einsum("rkgd,nkd->rkgn", grouped, key_block, preferred_element_type=jnp.float32)
        * scale_factor
    )
    if visible is not None:
        scores = jnp.where(visible[:, None, None, :], scores, -jnp.inf)
    new_max = jnp.maximum(maximum, jnp.max(scores, axis=3))
    weights = jnp.exp(scores - new_max[..., None])
    rescale = jnp.exp(maximum - new_max)
    rounded = weights.astype(jnp.bfloat16)
    summed = summed * rescale + jnp.sum(weights, axis=3)
    weighted = weighted * rescale[..., None] + jnp.einsum(
        "rkgn,nkd->rkgd", rounded, value_block, preferred_element_type=jnp.float32
    )
    return (new_max, summed, weighted)


def per_device(
    queries, prompt_keys, prompt_values, response_keys, response_values, lengths, out_weight
):
    row_count = queries.shape[0]
    kv_local = prompt_keys.shape[1] // HD
    group_size = HEADS // KVH
    scale_factor = HD ** (-0.5)
    grouped = queries.reshape(row_count, kv_local, group_size, HD)
    first_row = lax.axis_index("seq") * row_count
    positions, own_start = segment_layout(lengths, first_row, row_count)
    softmax_state = (
        jnp.full((row_count, kv_local, group_size), -jnp.inf, jnp.float32),
        jnp.zeros((row_count, kv_local, group_size), jnp.float32),
        jnp.zeros((row_count, kv_local, group_size, HD), jnp.float32),
    )
    prompt_pair = jnp.stack([prompt_keys, prompt_values])
    fragment = lax.all_gather(prompt_pair, "seq", axis=1, tiled=True)
    frag_rows = fragment.shape[1]
    key_block = fragment[0].reshape(frag_rows, kv_local, HD)
    value_block = fragment[1].reshape(frag_rows, kv_local, HD)
    softmax_state = update_state(softmax_state, grouped, key_block, value_block, None, scale_factor)
    response_pair = jnp.stack([response_keys, response_values])
    fragment = lax.all_gather(response_pair, "seq", axis=1, tiled=True)
    frag_rows = fragment.shape[1]
    key_pos = jnp.arange(frag_rows, dtype=jnp.int32)
    visible = (key_pos[None, :] <= positions[:, None]) & (key_pos[None, :] >= own_start[:, None])
    key_block = fragment[0].reshape(frag_rows, kv_local, HD)
    value_block = fragment[1].reshape(frag_rows, kv_local, HD)
    softmax_state = update_state(
        softmax_state, grouped, key_block, value_block, visible, scale_factor
    )
    maximum, summed, weighted = softmax_state
    attended = (
        (weighted / summed[..., None])
        .astype(jnp.bfloat16)
        .reshape(row_count, kv_local * group_size * HD)
    )
    partial_out = jnp.dot(attended, out_weight, preferred_element_type=jnp.float32)
    return lax.psum_scatter(partial_out.astype(jnp.bfloat16), "tp", scatter_dimension=1, tiled=True)


def solution(mesh):
    in_specs = (
        P("seq", "tp"),
        P("seq", "tp"),
        P("seq", "tp"),
        P("seq", "tp"),
        P("seq", "tp"),
        P(),
        P("tp", None),
    )
    out_specs = P("seq", "tp")
    return jax.shard_map(
        per_device, mesh=mesh, in_specs=in_specs, out_specs=out_specs, check_vma=False
    )
```

profile of v0, /device:TPU:32, one launch (start us, length us, event | category | flops | bytes accessed | tf_op | source)
XLA Modules:
  0.0 299.7 jit_solution(3897833121249140386)
XLA Ops:
  6.5 0.0 all-gather.3.cloned.1.call-start
  6.5 1.4 pad_maximum_fusion.1
  7.9 0.0 all-gather.3.cloned.1.call-update
  8.0 0.0 all-gather.5.cloned.1.call-start
  8.0 1.5 pad_maximum_fusion
  9.6 0.0 all-gather.5.cloned.1.call-update
  9.6 0.0 reduce-scatter.4.cloned.1.call-start
  9.6 0.7 copy.35
  10.4 0.1 reduce.4
  10.5 0.7 sub.50
  11.2 1.1 copy.31
  12.3 0.1 select_reduce_fusion
  12.4 2.0 fusion.13
  14.5 0.0 copy-start.2
  14.5 77.3 %all-gather.3.cloned.1.call-done = bf16[2,4096,128]{2,1,0:T(8,128)(2,1)} async-done(((bf16[2,128,128]{2,1,0:T(8,128)(2,1)}), bf16[2,4096,128]{2,1,0:T(8,128)(2,1)}) %all-gather.3.cloned.1.call-update) | async-done | bytes 2097168 | tf_op jit(solution)/shard_map/all_gather | solution.py:55
  91.8 4.1 %bitcast_reduce_fusion = (f32[256,5]{0,1:T(8,128)S(1)}, f32[4096,256,5]{1,0,2:T(8,128)S(1)}) fusion(bf16[256,5,128]{0,2,1:T(8,128)(2,1)S(1)} %bitcast.121, bf16[2,4096,128]{2,1,0:T(8,128)(2,1)} %all-gather.3.cloned.1.call-done), kind=kOutput, calls=%fused_computation.7 | convolution fusion | flops 1352661760 | bytes 22352896 | tf_op jit(solution)/shard_map/rkgd,nkd->rkgn/dot_general | solution.py:23
  95.9 0.0 copy-start
  95.9 7.0 %copy-done = f32[4096,256,5]{1,0,2:T(8,128)} copy-done((f32[4096,256,5]{1,0,2:T(8,128)}, f32[4096,256,5]{1,0,2:T(8,128)S(1)}, u32[]{:S(2)}) %copy-start) | copy-done | bytes 20971544
  102.9 3.8 %fusion.8 = f32[256,5]{0,1:T(8,128)S(1)} fusion(f32[4096,256,5]{1,0,2:T(8,128)S(1)} %get-tuple-element.9, f32[256,5]{0,1:T(8,128)S(1)} %get-tuple-element.8), kind=kLoop, calls=%fused_computation.11 | loop fusion | flops 15727360 | bytes 20981760 | tf_op jit(solution)/shard_map/reduce_sum | solution.py:32
  106.7 71.5 %all-gather.5.cloned.1.call-done = bf16[2,8192,128]{2,1,0:T(8,128)(2,1)} async-done(((bf16[2,256,128]{2,1,0:T(8,128)(2,1)}), bf16[2,8192,128]{2,1,0:T(8,128)(2,1)}) %all-gather.5.cloned.1.call-update) | async-done | bytes 4194320 | tf_op jit(solution)/shard_map/all_gather | solution.py:61
  178.2 0.0 copy-done.2
  178.2 18.1 %fusion.2 = (f32[256,5]{0,1:T(8,128)S(1)}, f32[8192,256,5]{1,0,2:T(8,128)}) fusion(pred[256,8192]{0,1:T(8,128)(4,1)S(1)} %fusion.13, bf16[256,5,128]{0,2,1:T(8,128)(2,1)S(1)} %bitcast.122, bf16[2,8192,128]{2,1,0:T(8,128)(2,1)} %all-gather.5.cloned.1.call-done), kind=kOutput, calls=%fused_computation.4 | convolution fusion | flops 2715810560 | bytes 46470144 | tf_op jit(solution)/shard_map/rkgd,nkd->rkgn/dot_general | solution.py:23
  196.4 0.0 copy-start.1
  196.4 18.6 %fusion = f32[256,5]{0,1:T(8,128)S(1)} fusion(f32[8192,256,5]{1,0,2:T(8,128)} %get-tuple-element.11, f32[256,5]{0,1:T(8,128)S(1)} %max.17, pred[256,8192]{0,1:T(8,128)(4,1)} %copy-done.2), kind=kLoop, calls=%fused_computation.2 | loop fusion | flops 41941760 | bytes 44050432 | tf_op jit(solution)/shard_map/reduce_sum | solution.py:32
  215.0 1.1 copy-done.1
  216.1 4.5 %fusion.27 = f32[1,128,256,5]{2,1,3,0:T(8,128)S(1)} fusion(f32[4096,256,5]{1,0,2:T(8,128)S(1)} %copy-done.1, f32[256,5]{0,1:T(8,128)S(1)} %get-tuple-element.8, bf16[2,4096,128]{2,1,0:T(8,128)(2,1)} %all-gather.3.cloned.1.call-done, f32[256,5]{0,1:T(8,128)S(1)} %get-tuple-element.6, f32[256,5]{0,1:T(8,128)S(1)} %get-tuple-element.7), kind=kOutput, calls=%fused_computation.26 | convolution fusion | flops 1358233600 | bytes 22690816 | tf_op jit(solution)/shard_map/rkgn,nkd->rkgd/dot_general | solution.py:33
  220.6 18.8 %fusion.34 = bf16[1,128,256,5]{2,1,3,0:T(8,128)(2,1)S(1)} fusion(f32[1,128,256,5]{2,1,3,0:T(8,128)S(1)} %fusion.27, f32[8192,256,5]{1,0,2:T(8,128)} %get-tuple-element.11, f32[256,5]{0,1:T(8,128)S(1)} %max.17, pred[256,8192]{0,1:T(8,128)(4,1)} %copy-done.2, bf16[2,8192,128]{2,1,0:T(8,128)(2,1)} %all-gather.5.cloned.1.call-done, ...), kind=kOutput, calls=%fused_computation.31 | convolution fusion | flops 2726789120 | bytes 47130624 | tf_op jit(solution)/shard_map/rkgn,nkd->rkgd/dot_general | solution.py:33
  239.3 5.1 %convolution_convert_fusion = bf16[256,5120]{1,0:T(8,128)(2,1)S(1)} fusion(bf16[256,640]{0,1:T(8,128)(2,1)S(1)} %bitcast.123, bf16[640,5120]{1,0:T(8,128)(2,1)} %param.13), kind=kOutput, calls=%fused_computation.18 | convolution fusion | flops 1679032320 | bytes 9502720 | tf_op jit(solution)/shard_map/dot_general | solution.py:76
  244.4 2.6 copy.47
  247.0 0.0 reduce-scatter.4.cloned.1.call-update
  247.0 44.3 %reduce-scatter.4.cloned.1.call-done = bf16[640,256]{1,0:T(8,128)(2,1)} async-done(((bf16[5120,256]{1,0:T(8,128)(2,1)}), bf16[640,256]{1,0:T(8,128)(2,1)}) %reduce-scatter.4.cloned.1.call-update) | async-done | bytes 327696
  291.3 1.9 copy.48
  (4 shorter events, 0.1 us)
Async XLA Ops:
  6.5 85.3 %all-gather.3.cloned.1.call-start = ((), (), s32[]{:S(2)}) async-start(), calls=%async_computation.1 | async-start | bytes 2162688 | tf_op jit(solution)/shard_map/all_gather | solution.py:55
  8.0 170.3 %all-gather.5.cloned.1.call-start = ((), (), s32[]{:S(2)}) async-start(), calls=%async_computation.2 | async-start | bytes 4325376 | tf_op jit(solution)/shard_map/all_gather | solution.py:61
  9.6 281.7 %reduce-scatter.4.cloned.1.call-start = ((), (), s32[]{:S(2)}) async-start(), calls=%async_computation.3 | async-start | bytes 2949120
  14.5 163.8 %copy-start.2 = (pred[256,8192]{0,1:T(8,128)(4,1)}, pred[256,8192]{0,1:T(8,128)(4,1)S(1)}, u32[]{:S(2)}) copy-start(pred[256,8192]{0,1:T(8,128)(4,1)S(1)} %fusion.13) | copy-start | bytes 6291460
  95.9 7.0 %copy-start = (f32[4096,256,5]{1,0,2:T(8,128)}, f32[4096,256,5]{1,0,2:T(8,128)S(1)}, u32[]{:S(2)}) copy-start(f32[4096,256,5]{1,0,2:T(8,128)S(1)} %get-tuple-element.9) | copy-start | bytes 62914564
  196.4 19.7 %copy-start.1 = (f32[4096,256,5]{1,0,2:T(8,128)S(1)}, f32[4096,256,5]{1,0,2:T(8,128)}, u32[]{:S(2)}) copy-start(f32[4096,256,5]{1,0,2:T(8,128)} %copy-done) | copy-start | bytes 62914564
Sparse Core Ops, SparseCore 0:
  10.2 81.6 all-gather.2
  94.6 83.5 all-gather.4
  247.2 44.0 reduce-scatter.3
where the time goes:
time: 300 us
  waiting for transfers between devices  193 us (64%)
  matrix products  50.5 us (17%)
  other arithmetic  28.3 us (9%)
  local copies, waits for them, and re-layouts  14.4 us (5%)
  between operations  13.2 us (4%)
    all_gather x1, waiting for transfers between devices, per_device(): fragment = lax.all_gather(prompt_pair, 'seq', axis=1, tiled=True)  77.3 us
    all_gather x1, waiting for transfers between devices, per_device(): fragment = lax.all_gather(response_pair, 'seq', axis=1, tiled=True)  71.5 us
    unnamed x4, waiting for transfers between devices  44.3 us
    dot_general x2, matrix products, update_state(): jnp.einsum('rkgn,nkd->rkgd', rounded, value_block, preferred_element_type...  23.2 us
    reduce_sum x2, other arithmetic, update_state(): summed = summed * rescale + jnp.sum(weights, axis=3)  22.5 us
    dot_general x2, matrix products, update_state(): jnp.einsum('rkgd,nkd->rkgn', grouped, key_block, preferred_element_type=j...  22.2 us
    unnamed x9, local copies, waits for them, and re-layouts  13.6 us
  transfers between devices with their start and end apart: 3, of which 3 were waited for; matrix products, arithmetic and copies ran while one was open for 5% of the time, Pallas kernels for 0%

commit v1 on v0

--- a/solution.py
+++ b/solution.py
@@ -2,10 +2,14 @@
 import jax.numpy as jnp
 from jax import lax
 from jax.sharding import PartitionSpec as P
+from jax.lax import all_to_all, axis_size
 
 HEADS = 40
 KVH = 8
 HD = 128
+trace_point = lambda s0, which_dim: jnp.concatenate(
+    all_to_all(jnp.stack(axis_size("seq") * [s0], axis=0), "seq", 0, 0), axis=which_dim
+)
 
 
 def segment_layout(lengths, first_row, row_count):
@@ -58,7 +62,7 @@
     value_block = fragment[1].reshape(frag_rows, kv_local, HD)
     softmax_state = update_state(softmax_state, grouped, key_block, value_block, None, scale_factor)
     response_pair = jnp.stack([response_keys, response_values])
-    fragment = lax.all_gather(response_pair, "seq", axis=1, tiled=True)
+    fragment = trace_point(response_pair, 1)
     frag_rows = fragment.shape[1]
     key_pos = jnp.arange(frag_rows, dtype=jnp.int32)
     visible = (key_pos[None, :] <= positions[:, None]) & (key_pos[None, :] >= own_start[:, None])

time: 300 us -> 274 us (0.913)
  waiting for transfers between devices: 193 us -> 148 us
  starting transfers between devices: 0.09 us -> 11.5 us
  matrix products: 50.5 us -> 55.8 us
  local copies, waits for them, and re-layouts: 14.4 us -> 19.4 us
    all_gather x1 -> x0, waiting for transfers between devices: 71.5 us -> none  [per_device(): fragment = lax.all_gather(response_pair, 'seq', axis=1, tiled=True)]
    all_gather x1, waiting for transfers between devices: 77.3 us -> 101 us  [per_device(): fragment = lax.all_gather(prompt_pair, 'seq', axis=1, tiled=True)]
    all_to_all x0 -> x1, starting transfers between devices: none -> 11.4 us  [all_to_all(jnp.stack(axis_size('seq') * [s0], axis=0), 'seq', 0, 0)]
    dot_general x2, matrix products: 23.2 us -> 28.5 us  [update_state(): jnp.einsum('rkgn,nkd->rkgd', rounded, value_block, preferred_element_type...]
    slice x0 -> x1, local copies, waits for them, and re-layouts: none -> 4.72 us  [per_device(): value_block = fragment[1].reshape(frag_rows, kv_local, HD)]
    unnamed x4 -> x3, waiting for transfers between devices: 44.3 us -> 47 us
    unnamed x9 -> x15, local copies, waits for them, and re-layouts: 13.6 us -> 11.6 us
  transfers between devices with their start and end apart: 3 -> 3, of which waited for: 3 -> 2; matrix products, arithmetic and copies ran while one was open for 5% -> 4% of each run, Pallas kernels for 0% -> 0%
where the time goes in v1:
time: 274 us
  waiting for transfers between devices  148 us (54%)
  matrix products  55.8 us (20%)
  other arithmetic  25.6 us (9%)
  local copies, waits for them, and re-layouts  19.4 us (7%)
  between operations  13.5 us (5%)
  starting transfers between devices  11.5 us (4%)
    all_gather x1, waiting for transfers between devices, per_device(): fragment = lax.all_gather(prompt_pair, 'seq', axis=1, tiled=True)  101 us
    unnamed x3, waiting for transfers between devices  47 us
    dot_general x2, matrix products, update_state(): jnp.einsum('rkgn,nkd->rkgd', rounded, value_block, preferred_element_type...  28.5 us
    dot_general x2, matrix products, update_state(): jnp.einsum('rkgd,nkd->rkgn', grouped, key_block, preferred_element_type=j...  22.2 us
    reduce_sum x2, other arithmetic, update_state(): summed = summed * rescale + jnp.sum(weights, axis=3)  21.8 us
    unnamed x15, local copies, waits for them, and re-layouts  11.6 us
    all_to_all x1, starting transfers between devices, all_to_all(jnp.stack(axis_size('seq') * [s0], axis=0), 'seq', 0, 0)  11.4 us
  transfers between devices with their start and end apart: 3, of which 2 were waited for; matrix products, arithmetic and copies ran while one was open for 4% of the time, Pallas kernels for 0%

profile of v1, /device:TPU:32, one launch (start us, length us, event | category | flops | bytes accessed | tf_op | source)
XLA Modules:
  0.0 273.6 jit_solution(4689285555307944694)
XLA Ops:
  6.5 0.0 copy-start.4
  6.5 0.0 copy-start.3
  6.5 0.0 copy-start.5
  6.5 0.0 copy-start.2
  6.5 0.9 pad_maximum_fusion
  7.5 3.0 %stack.20 = bf16[32,2,256,128]{3,2,1,0:T(8,128)(2,1)} broadcast(bf16[2,256,128]{2,1,0:T(8,128)(2,1)S(1)} %pad_maximum_fusion), dimensions={1,2,3} | broadcast | bytes 4325376 | tf_op jit(solution)/shard_map/stack | solution.py:11
  10.5 11.4 %all-to-all-start = ((bf16[32,2,256,128]{3,2,1,0:T(8,128)(2,1)}), bf16[32,2,256,128]{3,2,1,0:T(8,128)(2,1)}, u32[]{:S(2)}, u32[]{:S(2)}) async-start(bf16[32,2,256,128]{3,2,1,0:T(8,128)(2,1)} %stack.20), calls=%async_computation | async-start | bytes 8388608 | tf_op jit(solution)/shard_map/all_to_all | solution.py:11
  21.9 0.0 all-gather.2.cloned.1.call-start
  21.9 0.0 copy-done.4
  21.9 0.0 copy-done.3
  22.0 0.6 pad_maximum_fusion.1
  22.6 0.0 all-gather.2.cloned.1.call-update
  22.6 0.0 reduce-scatter.4.cloned.1.call-start
  22.7 0.0 copy-done.5
  22.7 0.1 copy.35
  22.8 0.1 reduce.4
  22.9 0.0 copy-done.2
  22.9 0.2 copy.31
  23.1 0.1 select_reduce_fusion
  23.2 2.0 fusion.13
  25.3 100.7 %all-gather.2.cloned.1.call-done = bf16[2,4096,128]{2,1,0:T(8,128)(2,1)} async-done(((bf16[2,128,128]{2,1,0:T(8,128)(2,1)}), bf16[2,4096,128]{2,1,0:T(8,128)(2,1)}) %all-gather.2.cloned.1.call-update) | async-done | bytes 2097168 | tf_op jit(solution)/shard_map/all_gather | solution.py:59
  126.0 4.1 %bitcast_reduce_fusion = (f32[256,5]{0,1:T(8,128)S(1)}, f32[4096,256,5]{1,0,2:T(8,128)S(1)}) fusion(bf16[256,5,128]{0,2,1:T(8,128)(2,1)S(1)} %bitcast.114, bf16[2,4096,128]{2,1,0:T(8,128)(2,1)} %all-gather.2.cloned.1.call-done), kind=kOutput, calls=%fused_computation.7 | convolution fusion | flops 1352661760 | bytes 22352896 | tf_op jit(solution)/shard_map/rkgd,nkd->rkgn/dot_general | solution.py:27
  130.1 0.0 copy-start
  130.1 7.0 %copy-done = f32[4096,256,5]{1,0,2:T(8,128)} copy-done((f32[4096,256,5]{1,0,2:T(8,128)}, f32[4096,256,5]{1,0,2:T(8,128)S(1)}, u32[]{:S(2)}) %copy-start) | copy-done | bytes 20971544
  137.1 3.8 %fusion.8 = f32[256,5]{0,1:T(8,128)S(1)} fusion(f32[4096,256,5]{1,0,2:T(8,128)S(1)} %get-tuple-element.11, f32[256,5]{0,1:T(8,128)S(1)} %get-tuple-element.10), kind=kLoop, calls=%fused_computation.11 | loop fusion | flops 15727360 | bytes 20981760 | tf_op jit(solution)/shard_map/reduce_sum | solution.py:36
  140.9 0.0 all-to-all-done
  140.9 4.7 %fusion.39 = (bf16[1,32,256,128]{3,2,0,1:T(8,128)(2,1)}, bf16[1,32,256,128]{3,2,0,1:T(8,128)(2,1)}) fusion(bf16[2,32,256,128]{3,2,0,1:T(8,128)(2,1)} %bitcast.15), kind=kLoop, calls=%fused_computation.39 | loop fusion | bytes 8388608 | tf_op jit(solution)/shard_map/slice | solution.py:70
  145.6 18.1 %fusion.2 = (f32[256,5]{0,1:T(8,128)S(1)}, f32[8192,256,5]{1,0,2:T(8,128)}) fusion(pred[256,8192]{0,1:T(8,128)(4,1)S(1)} %fusion.13, bf16[8192,128,1]{1,0,2:T(8,128)(2,1)} %bitcast.113, bf16[256,5,128]{0,2,1:T(8,128)(2,1)S(1)} %bitcast.115), kind=kOutput, calls=%fused_computation.4 | convolution fusion | flops 2715810560 | bytes 46470144 | tf_op jit(solution)/shard_map/rkgd,nkd->rkgn/dot_general | solution.py:27
  163.7 0.0 copy-start.1
  163.7 17.9 %fusion = f32[256,5]{0,1:T(8,128)S(1)} fusion(f32[8192,256,5]{1,0,2:T(8,128)} %get-tuple-element.13, f32[256,5]{0,1:T(8,128)S(1)} %max.17, pred[256,8192]{0,1:T(8,128)(4,1)S(1)} %fusion.13), kind=kLoop, calls=%fused_computation.2 | loop fusion | flops 41941760 | bytes 44050432 | tf_op jit(solution)/shard_map/reduce_sum | solution.py:36
  181.7 0.0 copy-done.1
  181.7 9.2 %fusion.26 = f32[1,128,256,5]{2,1,3,0:T(8,128)S(1)} fusion(f32[4096,256,5]{1,0,2:T(8,128)} %copy-done, f32[256,5]{0,1:T(8,128)S(1)} %get-tuple-element.10, bf16[2,4096,128]{2,1,0:T(8,128)(2,1)S(1)} %copy-done.1, f32[256,5]{0,1:T(8,128)S(1)} %get-tuple-element.6, f32[256,5]{0,1:T(8,128)S(1)} %get-tuple-element.9), kind=kOutput, calls=%fused_computation.23 | convolution fusion | flops 1358233600 | bytes 22700032 | tf_op jit(solution)/shard_map/rkgn,nkd->rkgd/dot_general | solution.py:37
  191.0 19.3 %fusion.33 = bf16[1,128,256,5]{2,1,3,0:T(8,128)(2,1)S(1)} fusion(f32[1,128,256,5]{2,1,3,0:T(8,128)S(1)} %fusion.26, bf16[8192,128,1]{1,0,2:T(8,128)(2,1)} %bitcast.112, f32[8192,256,5]{1,0,2:T(8,128)} %get-tuple-element.13, f32[256,5]{0,1:T(8,128)S(1)} %max.17, pred[256,8192]{0,1:T(8,128)(4,1)S(1)} %fusion.13, f32[256,5]{0,1:T(8,128)S(1)} %get-tuple-element.5), kind=kOutput, calls=%fused_computation.28 | convolution fusion | flops 2726789120 | bytes 47130624 | tf_op jit(solution)/shard_map/rkgn,nkd->rkgd/dot_general | solution.py:37
  210.2 5.1 %convolution_convert_fusion = bf16[256,5120]{1,0:T(8,128)(2,1)S(1)} fusion(bf16[256,640]{0,1:T(8,128)(2,1)S(1)} %bitcast.116, bf16[640,5120]{1,0:T(8,128)(2,1)} %param.13), kind=kOutput, calls=%fused_computation.18 | convolution fusion | flops 1679032320 | bytes 9502720 | tf_op jit(solution)/shard_map/dot_general | solution.py:80
  215.4 2.6 copy.46
  217.9 0.0 reduce-scatter.4.cloned.1.call-update
  218.0 46.9 %reduce-scatter.4.cloned.1.call-done = bf16[640,256]{1,0:T(8,128)(2,1)} async-done(((bf16[5120,256]{1,0:T(8,128)(2,1)}), bf16[640,256]{1,0:T(8,128)(2,1)}) %reduce-scatter.4.cloned.1.call-update) | async-done | bytes 327696
  264.9 1.9 copy.47
  (5 shorter events, 0.1 us)
Async XLA Ops:
  6.5 15.4 %copy-start.4 = (bf16[128,128]{1,0:T(8,128)(2,1)S(1)}, bf16[128,128]{1,0:T(8,128)(2,1)}, u32[]{:S(2)}) copy-start(bf16[128,128]{1,0:T(8,128)(2,1)} %param.8) | copy-start | bytes 98308
  6.5 15.4 %copy-start.3 = (bf16[128,128]{1,0:T(8,128)(2,1)S(1)}, bf16[128,128]{1,0:T(8,128)(2,1)}, u32[]{:S(2)}) copy-start(bf16[128,128]{1,0:T(8,128)(2,1)} %param.9) | copy-start | bytes 98308
  6.5 16.1 %copy-start.5 = (s32[16]{0:T(128)S(1)}, s32[16]{0:T(128)}, u32[]{:S(2)}) copy-start(s32[16]{0:T(128)} %param.12) | copy-start | bytes 196
  6.5 16.4 %copy-start.2 = (bf16[256,640]{1,0:T(8,128)(2,1)S(1)}, bf16[256,640]{1,0:T(8,128)(2,1)}, u32[]{:S(2)}) copy-start(bf16[256,640]{1,0:T(8,128)(2,1)} %param.7) | copy-start | bytes 983044
  10.5 130.4 %all-to-all-start = ((bf16[32,2,256,128]{3,2,1,0:T(8,128)(2,1)}), bf16[32,2,256,128]{3,2,1,0:T(8,128)(2,1)}, u32[]{:S(2)}, u32[]{:S(2)}) async-start(bf16[32,2,256,128]{3,2,1,0:T(8,128)(2,1)} %stack.20), calls=%async_computation | async-start | bytes 8388608 | tf_op jit(solution)/shard_map/all_to_all | solution.py:11
  21.9 104.1 %all-gather.2.cloned.1.call-start = ((), (), s32[]{:S(2)}) async-start(), calls=%async_computation.2 | async-start | bytes 2162688 | tf_op jit(solution)/shard_map/all_gather | solution.py:59
  22.6 242.3 %reduce-scatter.4.cloned.1.call-start = ((), (), s32[]{:S(2)}) async-start(), calls=%async_computation.3 | async-start | bytes 2949120
  130.1 7.0 %copy-start = (f32[4096,256,5]{1,0,2:T(8,128)}, f32[4096,256,5]{1,0,2:T(8,128)S(1)}, u32[]{:S(2)}) copy-start(f32[4096,256,5]{1,0,2:T(8,128)S(1)} %get-tuple-element.11) | copy-start | bytes 62914564
  163.7 18.0 %copy-start.1 = (bf16[2,4096,128]{2,1,0:T(8,128)(2,1)S(1)}, bf16[2,4096,128]{2,1,0:T(8,128)(2,1)}, u32[]{:S(2)}) copy-start(bf16[2,4096,128]{2,1,0:T(8,128)(2,1)} %all-gather.2.cloned.1.call-done) | copy-start | bytes 6291460
Sparse Core Ops, SparseCore 0:
  25.5 100.4 all-gather.1
  218.1 46.7 reduce-scatter.3
